TPU v7x, 32 devices: a whole 2x2x4 slice. The times are simulated.
32 devices in a mesh: mem: 8 (over z, y), lat: 4 (over x, core).
Axes of the slice: x: 2, y: 2, z: 4, core: 2. Of those that a mesh axis runs over, the one named last changes fastest.
Arguments:
- prior_sample_states: bfloat16 [16, 2, 16, 1024], P('mem', None, 'lat'), may hold values from -6 to 6
- wind_cfl_ratios: float32 [2, 16, 1024], P(None, 'lat'), may hold values from -0.45 to 0.45
- obs_cell: int32 [4, 2048], P('lat', 'mem'), may hold values from 0 to 511
- obs_value: float32 [4, 2048], P('lat', 'mem'), may hold values from -6 to 6
- obs_precision: float32 [4, 2048], P('lat', 'mem'), may hold values from 0.25 to 4
- neighbours: int32 [16, 8, 512], P('lat', 'mem'), may hold values from 0 to 1279, as said below
- obs_counts: int32 [16, 8], P('lat', 'mem'), may hold values from 128 to 512, as said below
Outputs:
- analysis: bfloat16 [16, 2, 16, 1024], P('mem', None, 'lat')
Inputs may be any that keep to these rules, and one draw needn't show every extreme that they name: `obs_counts`: in every tile some block's list has all 512 slots live. `neighbours`: the 512 entries of one list are distinct and index the extended set of its tile.
All inputs are finite; a program needn't handle non-finite values. Where the computation divides by a largest or mean magnitude, that divisor is 1e-20 or more.
Results may differ from a plain program's by a relative error of at most 0.0053.
Values may be sent and summed in bfloat16 or wider, within the bound.
A program may use at most 64 MiB of HBM per device.

v0:
```python
import jax
import jax.numpy as jnp
from jax import lax
from jax.sharding import PartitionSpec as P

PATCH_WIDTH = 128
SECTIONS = 4
NS_ITERS = 6
LOC_ROWS = 2
LOC_COLS = 64
KAPPA = (0.025, 0.0125)
HIGHEST = lax.Precision.HIGHEST


def with_halo(cells, sides, width):
    for axis, dim in sides:
        count = lax.axis_size(axis)
        ends = count - 1
        head = lax.slice_in_dim(cells, 0, width, axis=dim)
        tail = lax.slice_in_dim(cells, cells.shape[dim] - width, cells.shape[dim], axis=dim)
        cells = jnp.concatenate(
            [
                lax.ppermute(tail, axis, [(i, (i + 1) % count) for i in range(ends)]),
                cells,
                lax.ppermute(head, axis, [((i + 1) % count, i) for i in range(ends)]),
            ],
            axis=dim,
        )
    return cells


def advance(padded, east_wind, north_wind, diffusion):
    centre = padded[:, 1:-1, :]
    north_row = padded[:, 2:, :]
    south_row = padded[:, :-2, :]
    widened = jnp.pad(centre, ((0, 0), (0, 0), (1, 1)))
    west_cell = widened[:, :, :-2]
    east_cell = widened[:, :, 2:]
    transport = (
        jnp.maximum(east_wind, 0.0) * (centre - west_cell)
        + jnp.minimum(east_wind, 0.0) * (east_cell - centre)
        + jnp.maximum(north_wind, 0.0) * (centre - south_row)
        + jnp.minimum(north_wind, 0.0) * (north_row - centre)
    )
    return (
        centre
        - transport
        + diffusion * (north_row + south_row + east_cell + west_cell - 4.0 * centre)
    )


def place_piece(piece, sample_realizations, row_shift, col_shift):
    return jnp.concatenate(
        [
            piece[: sample_realizations + 2],
            piece[sample_realizations + 2 : sample_realizations + 3] + row_shift,
            piece[sample_realizations + 3 :] + col_shift,
        ],
        axis=0,
    )


def analyze(mesh_patch, extended, block_lists, block_counts):
    sample_realizations = mesh_patch.shape[0]
    analysis_block_count = mesh_patch.shape[2]
    tile_width = mesh_patch.shape[3]
    extent = extended.shape[1]
    slot_count = block_lists.shape[1]
    obs_ens = extended[:sample_realizations]
    obs_mean = jnp.mean(obs_ens, axis=0)
    spread = obs_ens - obs_mean
    innovation = extended[sample_realizations] - obs_mean
    precision = extended[sample_realizations + 1]
    obs_row = extended[sample_realizations + 2]
    obs_col = extended[sample_realizations + 3]
    active = (jnp.arange(slot_count, dtype=jnp.int32)[None, :] < block_counts[:, None]).astype(
        jnp.float32
    )
    block_ids = jnp.broadcast_to(
        jnp.arange(analysis_block_count, dtype=jnp.int32)[:, None], block_lists.shape
    )
    membership = (
        jnp.zeros((analysis_block_count, extent), jnp.float32)
        .at[block_ids, block_lists]
        .set(active)
    )
    block_row = jnp.arange(analysis_block_count, dtype=jnp.float32)[:, None]
    row_gap = obs_row[None, :] - block_row
    col_gap = obs_col[None, :] - 0.5 * (tile_width - 1)
    tapering = jnp.exp(-0.5 * ((row_gap / LOC_ROWS) ** 2 + (col_gap / LOC_COLS) ** 2))
    weight = membership * tapering * precision[None, :]
    weighted = spread[None, :, :] * weight[:, None, :]
    gram_matrix = jnp.einsum("rek,fk->ref", weighted, spread, precision=HIGHEST)
    forcing = jnp.einsum("ek,rk->re", spread, weight * innovation[None, :], precision=HIGHEST)
    identity = jnp.eye(sample_realizations, dtype=jnp.float32)
    system = (sample_realizations - 1.0) * identity + gram_matrix
    bounds = sample_realizations - 1.0 + jnp.max(jnp.sum(jnp.abs(gram_matrix), axis=2), axis=1)
    upper_iter = system / bounds[:, None, None]
    lower_iter = jnp.broadcast_to(identity, system.shape)
    for iteration in range(NS_ITERS):
        factor = 1.5 * identity - 0.5 * jnp.einsum(
            "rij,rjk->rik", lower_iter, upper_iter, precision=HIGHEST
        )
        upper_iter = jnp.einsum("rij,rjk->rik", upper_iter, factor, precision=HIGHEST)
        lower_iter = jnp.einsum("rij,rjk->rik", factor, lower_iter, precision=HIGHEST)
    inv_root = lower_iter / jnp.sqrt(bounds)[:, None, None]
    half_shift = jnp.einsum("rij,rj->ri", inv_root, forcing, precision=HIGHEST)
    mean_shift = jnp.einsum("rij,rj->ri", inv_root, half_shift, precision=HIGHEST)
    weights = jnp.sqrt(sample_realizations - 1.0) * inv_root + mean_shift[:, :, None]
    fields = mesh_patch.astype(jnp.float32)
    centre = jnp.mean(fields, axis=0)
    anomalies = fields - centre
    updated = centre + jnp.einsum("kvrc,rkm->mvrc", anomalies, weights, precision=HIGHEST)
    return updated.astype(jnp.bfloat16)


def on_device(
    prior_sample_states, wind_cfl_ratios, obs_cell, obs_value, obs_precision, neighbours, obs_counts
):
    ensemble_count = prior_sample_states.shape[0]
    analysis_block_count = prior_sample_states.shape[2]
    longitude_index = prior_sample_states.shape[3]
    present_states = prior_sample_states.astype(jnp.float32).reshape(
        ensemble_count * 2, analysis_block_count, longitude_index
    )
    diffusion = jnp.tile(jnp.array(KAPPA, jnp.float32).reshape(2, 1, 1), (ensemble_count, 1, 1))
    for section_index in range(SECTIONS):
        padded = with_halo(present_states, (("lat", 1),), 1)
        present_states = advance(padded, wind_cfl_ratios[0], wind_cfl_ratios[1], diffusion)
    predict_advance = present_states.astype(jnp.bfloat16).reshape(
        ensemble_count, 2, analysis_block_count, longitude_index
    )
    cells = obs_cell[0]
    own_meta = jnp.stack(
        [
            obs_value[0],
            obs_precision[0],
            (cells // PATCH_WIDTH).astype(jnp.float32),
            (cells % PATCH_WIDTH).astype(jnp.float32),
        ],
        axis=0,
    )
    mesh_patches = lax.all_to_all(predict_advance, "mem", split_axis=3, concat_axis=0, tiled=True)
    sample_realizations = mesh_patches.shape[0]
    own_obs = jnp.take(mesh_patches[:, 0].reshape(sample_realizations, -1), cells, axis=1).astype(
        jnp.float32
    )
    combined = jnp.concatenate([own_obs, own_meta], axis=0)
    beside_all = with_halo(combined[None, None], (("mem", 1), ("lat", 0)), 1)
    pieces = [
        beside_all[1, 1],
        beside_all[0, 1],
        beside_all[2, 1],
        beside_all[1, 0],
        beside_all[1, 2],
    ]
    row_span = float(analysis_block_count)
    col_span = float(PATCH_WIDTH)
    shifts = [(0.0, 0.0), (-row_span, 0.0), (row_span, 0.0), (0.0, -col_span), (0.0, col_span)]
    extended = jnp.concatenate(
        [
            place_piece(pieces[slot], sample_realizations, shifts[slot][0], shifts[slot][1])
            for slot in range(5)
        ],
        axis=1,
    )
    updated = analyze(mesh_patches, extended, neighbours[:, 0, :], obs_counts[:, 0])
    return lax.all_to_all(updated, "mem", split_axis=0, concat_axis=3, tiled=True)


def solution(mesh):
    placed = (
        P("mem", None, "lat", None),
        P(None, "lat", None),
        P("lat", "mem"),
        P("lat", "mem"),
        P("lat", "mem"),
        P("lat", "mem", None),
        P("lat", "mem"),
    )
    return jax.shard_map(
        on_device,
        mesh=mesh,
        in_specs=placed,
        out_specs=P("mem", None, "lat", None),
        check_vma=False,
    )
```

profile of v0, /device:TPU:1, one launch (start us, length us, event | category | flops | bytes accessed | tf_op | source)
XLA Modules:
  0.0 93.3 jit_solution(944328057822813094)
XLA Ops:
  0.0 0.8 bitcast_convert_fusion
  0.8 4.5 %collective-permute-start = (f32[4,1,1024]{2,0,1:T(4,128)S(1)}, f32[4,1,1024]{2,0,1:T(4,128)S(1)}, u32[]{:S(2)}, u32[]{:S(2)}) collective-permute-start(f32[4,1,1024]{2,0,1:T(4,128)S(1)} %get-tuple-element.17), channel_id=1, source_target_pairs={{0,1},{1,2},{2,3},{4,5},{5,6},{6,7},{8,9},{9,10},{10,11},{12,13},{... | collective-permute-start | bytes 49160 | tf_op jit(solution)/shard_map/ppermute | solution.py:23
  5.4 1.9 %collective-permute-start.1 = (f32[4,1,1024]{2,0,1:T(4,128)S(1)}, f32[4,1,1024]{2,0,1:T(4,128)S(1)}, u32[]{:S(2)}, u32[]{:S(2)}) collective-permute-start(f32[4,1,1024]{2,0,1:T(4,128)S(1)} %get-tuple-element.18), channel_id=1, source_target_pairs={{1,0},{2,1},{3,2},{5,4},{6,5},{7,6},{9,8},{10,9},{11,10},{13,12},{... | collective-permute-start | bytes 49160 | tf_op jit(solution)/shard_map/ppermute | solution.py:25
  7.4 0.6 copy-done.2
  8.1 0.6 copy-done.6
  8.7 0.1 multiply_reduce_fusion
  8.8 0.6 copy-done.7
  9.4 0.1 and_reduce_fusion
  9.5 0.6 copy-done.5
  10.2 0.6 copy-done.8
  11.0 0.1 fusion.58
  11.1 3.6 %collective-permute-start.2 = (f32[4,1,1024]{2,0,1:T(4,128)S(1)}, f32[4,1,1024]{2,0,1:T(4,128)S(1)}, u32[]{:S(2)}, u32[]{:S(2)}) collective-permute-start(f32[4,1,1024]{2,0,1:T(4,128)S(1)} %get-tuple-element.15), channel_id=1, source_target_pairs={{0,1},{1,2},{2,3},{4,5},{5,6},{6,7},{8,9},{9,10},{10,11},{12,13},{... | collective-permute-start | bytes 49160 | tf_op jit(solution)/shard_map/ppermute | solution.py:23
  14.8 1.9 %collective-permute-start.3 = (f32[4,1,1024]{2,0,1:T(4,128)S(1)}, f32[4,1,1024]{2,0,1:T(4,128)S(1)}, u32[]{:S(2)}, u32[]{:S(2)}) collective-permute-start(f32[4,1,1024]{2,0,1:T(4,128)S(1)} %get-tuple-element.16), channel_id=1, source_target_pairs={{1,0},{2,1},{3,2},{5,4},{6,5},{7,6},{9,8},{10,9},{11,10},{13,12},{... | collective-permute-start | bytes 49160 | tf_op jit(solution)/shard_map/ppermute | solution.py:25
  16.7 3.1 %collective-permute-done.3 = f32[4,1,1024]{2,0,1:T(4,128)S(1)} collective-permute-done((f32[4,1,1024]{2,0,1:T(4,128)S(1)}, f32[4,1,1024]{2,0,1:T(4,128)S(1)}, u32[]{:S(2)}, u32[]{:S(2)}) %collective-permute-start.3) | collective-permute-done | bytes 16416 | tf_op jit(solution)/shard_map/ppermute | solution.py:25
  19.8 0.1 fusion.45
  20.0 1.9 %collective-permute-start.4 = (f32[4,1,1024]{2,0,1:T(4,128)S(1)}, f32[4,1,1024]{2,0,1:T(4,128)S(1)}, u32[]{:S(2)}, u32[]{:S(2)}) collective-permute-start(f32[4,1,1024]{2,0,1:T(4,128)S(1)} %get-tuple-element.13), channel_id=1, source_target_pairs={{0,1},{1,2},{2,3},{4,5},{5,6},{6,7},{8,9},{9,10},{10,11},{12,13},{... | collective-permute-start | bytes 49160 | tf_op jit(solution)/shard_map/ppermute | solution.py:23
  21.9 2.4 %collective-permute-start.5 = (f32[4,1,1024]{2,0,1:T(4,128)S(1)}, f32[4,1,1024]{2,0,1:T(4,128)S(1)}, u32[]{:S(2)}, u32[]{:S(2)}) collective-permute-start(f32[4,1,1024]{2,0,1:T(4,128)S(1)} %get-tuple-element.14), channel_id=1, source_target_pairs={{1,0},{2,1},{3,2},{5,4},{6,5},{7,6},{9,8},{10,9},{11,10},{13,12},{... | collective-permute-start | bytes 49160 | tf_op jit(solution)/shard_map/ppermute | solution.py:25
  24.4 2.6 %collective-permute-done.5 = f32[4,1,1024]{2,0,1:T(4,128)S(1)} collective-permute-done((f32[4,1,1024]{2,0,1:T(4,128)S(1)}, f32[4,1,1024]{2,0,1:T(4,128)S(1)}, u32[]{:S(2)}, u32[]{:S(2)}) %collective-permute-start.5) | collective-permute-done | bytes 16416 | tf_op jit(solution)/shard_map/ppermute | solution.py:25
  27.0 0.1 fusion.32
  27.2 1.9 %collective-permute-start.6 = (f32[4,1,1024]{2,0,1:T(4,128)S(1)}, f32[4,1,1024]{2,0,1:T(4,128)S(1)}, u32[]{:S(2)}, u32[]{:S(2)}) collective-permute-start(f32[4,1,1024]{2,0,1:T(4,128)S(1)} %get-tuple-element.11), channel_id=1, source_target_pairs={{0,1},{1,2},{2,3},{4,5},{5,6},{6,7},{8,9},{9,10},{10,11},{12,13},{... | collective-permute-start | bytes 49160 | tf_op jit(solution)/shard_map/ppermute | solution.py:23
  29.1 2.4 %collective-permute-start.7 = (f32[4,1,1024]{2,0,1:T(4,128)S(1)}, f32[4,1,1024]{2,0,1:T(4,128)S(1)}, u32[]{:S(2)}, u32[]{:S(2)}) collective-permute-start(f32[4,1,1024]{2,0,1:T(4,128)S(1)} %get-tuple-element.12), channel_id=1, source_target_pairs={{1,0},{2,1},{3,2},{5,4},{6,5},{7,6},{9,8},{10,9},{11,10},{13,12},{... | collective-permute-start | bytes 49160 | tf_op jit(solution)/shard_map/ppermute | solution.py:25
  31.5 8.1 %scatter_custom_fusion = f32[5120]{0:T(1024)S(1)} fusion(s32[2048]{0:T(1024)S(1)} %bitcast.143, f32[2048]{0:T(1024)S(1)} %bitcast.144, f32[]{:T(128)} %constant.37.clone.1), kind=kCustom, calls=%fused_computation.134 | custom fusion | bytes 20484
  39.8 0.2 fusion.67
  39.9 0.8 copy.122
  40.7 2.6 %reshape.227 = bf16[8,2,1024]{2,1,0:T(2,128)(2,1)} reshape(bf16[1024,2,2,4]{3,2,1,0:T(2,128)(2,1)S(1)} %bitcast.128) | data formatting | bytes 65536
  43.3 5.6 %all-to-all-start = ((bf16[8,2,1024]{2,1,0:T(2,128)(2,1)}), bf16[8,2,1024]{2,1,0:T(2,128)(2,1)S(1)}, u32[]{:S(2)}, u32[]{:S(2)}) async-start(bf16[8,2,1024]{2,1,0:T(2,128)(2,1)} %reshape.227), calls=%async_computation | async-start | bytes 65536 | tf_op jit(solution)/shard_map/all_to_all | solution.py:143
  48.9 5.6 %all-to-all-done = bf16[8,2,1024]{2,1,0:T(2,128)(2,1)S(1)} async-done(((bf16[8,2,1024]{2,1,0:T(2,128)(2,1)}), bf16[8,2,1024]{2,1,0:T(2,128)(2,1)S(1)}, u32[]{:S(2)}, u32[]{:S(2)}) %all-to-all-start) | async-done | bytes 32800 | tf_op jit(solution)/shard_map/all_to_all | solution.py:143
  54.5 2.2 %reshape.228 = bf16[1024,2,2,4]{3,2,1,0:T(2,128)(2,1)S(1)} reshape(bf16[8,2,1024]{2,1,0:T(2,128)(2,1)S(1)} %all-to-all-done) | data formatting | bytes 65536
  56.7 1.3 %copy.123 = bf16[2,2,4,8,128]{4,3,2,1,0:T(8,128)(2,1)S(1)} copy(bf16[2,2,4,8,128]{2,1,0,4,3:T(2,128)(2,1)S(1)} %bitcast.129) | data formatting | bytes 65536 | tf_op jit(solution)/shard_map/all_to_all | solution.py:143
  58.1 0.1 copy.124
  58.2 0.9 gather_fusion
  59.1 0.1 convert_bitcast_fusion
  59.2 0.6 copy-done.4
  60.0 2.3 %collective-permute-start.8 = (f32[1,1,20,256]{3,2,1,0:T(8,128)S(1)}, f32[1,1,20,256]{3,2,1,0:T(8,128)S(1)}, u32[]{:S(2)}, u32[]{:S(2)}) collective-permute-start(f32[1,1,20,256]{3,2,1,0:T(8,128)S(1)} %bitcast.132), channel_id=1, source_target_pairs={{0,4},{4,8},{8,12},{12,16},{16,20},{20,24},{24,28},{1,5},{5,9},{9,... | collective-permute-start | bytes 61448 | tf_op jit(solution)/shard_map/ppermute | solution.py:23
  62.3 1.3 %collective-permute-start.9 = (f32[1,1,20,256]{3,2,1,0:T(8,128)S(1)}, f32[1,1,20,256]{3,2,1,0:T(8,128)S(1)}, u32[]{:S(2)}, u32[]{:S(2)}) collective-permute-start(f32[1,1,20,256]{3,2,1,0:T(8,128)S(1)} %bitcast.133), channel_id=1, source_target_pairs={{4,0},{8,4},{12,8},{16,12},{20,16},{24,20},{28,24},{5,1},{9,5},{13... | collective-permute-start | bytes 61448 | tf_op jit(solution)/shard_map/ppermute | solution.py:25
  63.7 3.1 %collective-permute-done.9 = f32[1,1,20,256]{3,2,1,0:T(8,128)S(1)} collective-permute-done((f32[1,1,20,256]{3,2,1,0:T(8,128)S(1)}, f32[1,1,20,256]{3,2,1,0:T(8,128)S(1)}, u32[]{:S(2)}, u32[]{:S(2)}) %collective-permute-start.9) | collective-permute-done | bytes 20512 | tf_op jit(solution)/shard_map/ppermute | solution.py:25
  66.9 5.7 %collective-permute-start.10 = (f32[1,3,20,256]{3,0,2,1:T(1,128)S(1)}, f32[1,3,20,256]{3,0,2,1:T(1,128)S(1)}, u32[]{:S(2)}, u32[]{:S(2)}) collective-permute-start(f32[1,3,20,256]{3,0,2,1:T(1,128)S(1)} %copy_dynamic-update-slice_fusion), channel_id=1, source_target_pairs={{0,1},{1,2},{2,3},{4,5},{5,6},{6,7},{8,9},{9,10},{10,11},{12,13},{... | collective-permute-start | bytes 184328 | tf_op jit(solution)/shard_map/ppermute | solution.py:23
  72.6 1.9 %collective-permute-start.11 = (f32[1,3,20,256]{3,0,2,1:T(1,128)S(1)}, f32[1,3,20,256]{3,0,2,1:T(1,128)S(1)}, u32[]{:S(2)}, u32[]{:S(2)}) collective-permute-start(f32[1,3,20,256]{3,0,2,1:T(1,128)S(1)} %copy_dynamic-update-slice_fusion), channel_id=1, source_target_pairs={{1,0},{2,1},{3,2},{5,4},{6,5},{7,6},{9,8},{10,9},{11,10},{13,12},{... | collective-permute-start | bytes 184328 | tf_op jit(solution)/shard_map/ppermute | solution.py:25
  74.6 3.5 %collective-permute-done.11 = f32[1,3,20,256]{3,0,2,1:T(1,128)S(1)} collective-permute-done((f32[1,3,20,256]{3,0,2,1:T(1,128)S(1)}, f32[1,3,20,256]{3,0,2,1:T(1,128)S(1)}, u32[]{:S(2)}, u32[]{:S(2)}) %collective-permute-start.11) | collective-permute-done | bytes 61472 | tf_op jit(solution)/shard_map/ppermute | solution.py:25
  78.4 1.3 %abs_reduce_fusion = (f32[4,16]{1,0:T(4,128)S(1)}, f32[4,16,16]{1,2,0:T(8,128)S(1)}) fusion(f32[16,1280]{1,0:T(8,128)S(1)} %slice_subtract_fusion, f32[4,1280]{1,0:T(4,128)S(1)} %multiply_multiply_fusion), kind=kOutput, calls=%fused_computation.104 | convolution fusion | flops 15812544 | bytes 106752 | tf_op jit(solution)/shard_map/rek,fk->ref/dot_general | solution.py:93
  79.7 0.1 reduce_max.9
  79.8 0.3 fusion.7
  80.1 0.3 fusion.97
  80.4 0.2 fusion.76
  80.6 0.2 fusion.6
  80.7 0.2 fusion.103
  80.9 0.2 fusion.102
  81.1 0.2 fusion.5
  81.3 0.2 fusion.105
  81.4 0.2 fusion.104
  81.6 0.2 fusion.4
  81.8 0.2 fusion.107
  81.9 0.2 fusion.106
  82.1 0.2 fusion.3
  82.3 0.2 fusion.109
  82.5 0.2 fusion.108
  82.6 0.2 fusion.72
  82.8 0.2 fusion.2
  83.0 0.2 convolution_divide_fusion
  83.2 0.2 convolution_bitcast_fusion.1
  83.3 0.2 fusion.110
  83.5 0.3 fusion.1
  83.9 8.8 %all_to_all.36 = bf16[16,2,4,128]{3,1,2,0:T(2,128)(2,1)S(1)} all-to-all(bf16[16,2,4,128]{3,1,2,0:T(2,128)(2,1)S(1)} %copy.112), channel_id=1, replica_groups=mesh['mem'=8,'lat'=4] {'mem'}, dimensions={0} | all-to-all | bytes 65536 | tf_op jit(solution)/shard_map/all_to_all | solution.py:168
  92.7 0.6 all_to_all.33
  (78 shorter events, 1.1 us)
Async XLA Ops:
  0.8 6.5 %copy-start = (f32[2,4,1024]{2,1,0:T(4,128)S(1)}, f32[2,4,1024]{2,1,0:T(4,128)}, u32[]{:S(2)}) copy-start(f32[2,4,1024]{2,1,0:T(4,128)} %param.9) | copy-start | bytes 98308
  0.8 6.5 %copy-start.1 = (s32[1,256]{1,0:T(1,128)S(1)}, s32[1,256]{1,0:T(1,128)}, u32[]{:S(2)}) copy-start(s32[1,256]{1,0:T(1,128)} %param.10) | copy-start | bytes 3076
  0.8 10.1 %collective-permute-start = (f32[4,1,1024]{2,0,1:T(4,128)S(1)}, f32[4,1,1024]{2,0,1:T(4,128)S(1)}, u32[]{:S(2)}, u32[]{:S(2)}) collective-permute-start(f32[4,1,1024]{2,0,1:T(4,128)S(1)} %get-tuple-element.17), channel_id=1, source_target_pairs={{0,1},{1,2},{2,3},{4,5},{5,6},{6,7},{8,9},{9,10},{10,11},{12,13},{... | collective-permute-start | bytes 49160 | tf_op jit(solution)/shard_map/ppermute | solution.py:23
  5.4 5.6 %collective-permute-start.1 = (f32[4,1,1024]{2,0,1:T(4,128)S(1)}, f32[4,1,1024]{2,0,1:T(4,128)S(1)}, u32[]{:S(2)}, u32[]{:S(2)}) collective-permute-start(f32[4,1,1024]{2,0,1:T(4,128)S(1)} %get-tuple-element.18), channel_id=1, source_target_pairs={{1,0},{2,1},{3,2},{5,4},{6,5},{7,6},{9,8},{10,9},{11,10},{13,12},{... | collective-permute-start | bytes 49160 | tf_op jit(solution)/shard_map/ppermute | solution.py:25
  7.3 0.7 copy-start.2
  8.1 0.7 copy-start.6
  8.7 0.7 copy-start.7
  9.5 0.7 copy-start.5
  10.2 0.7 copy-start.8
  11.1 5.6 %collective-permute-start.2 = (f32[4,1,1024]{2,0,1:T(4,128)S(1)}, f32[4,1,1024]{2,0,1:T(4,128)S(1)}, u32[]{:S(2)}, u32[]{:S(2)}) collective-permute-start(f32[4,1,1024]{2,0,1:T(4,128)S(1)} %get-tuple-element.15), channel_id=1, source_target_pairs={{0,1},{1,2},{2,3},{4,5},{5,6},{6,7},{8,9},{9,10},{10,11},{12,13},{... | collective-permute-start | bytes 49160 | tf_op jit(solution)/shard_map/ppermute | solution.py:23
  14.8 5.1 %collective-permute-start.3 = (f32[4,1,1024]{2,0,1:T(4,128)S(1)}, f32[4,1,1024]{2,0,1:T(4,128)S(1)}, u32[]{:S(2)}, u32[]{:S(2)}) collective-permute-start(f32[4,1,1024]{2,0,1:T(4,128)S(1)} %get-tuple-element.16), channel_id=1, source_target_pairs={{1,0},{2,1},{3,2},{5,4},{6,5},{7,6},{9,8},{10,9},{11,10},{13,12},{... | collective-permute-start | bytes 49160 | tf_op jit(solution)/shard_map/ppermute | solution.py:25
  20.0 4.4 %collective-permute-start.4 = (f32[4,1,1024]{2,0,1:T(4,128)S(1)}, f32[4,1,1024]{2,0,1:T(4,128)S(1)}, u32[]{:S(2)}, u32[]{:S(2)}) collective-permute-start(f32[4,1,1024]{2,0,1:T(4,128)S(1)} %get-tuple-element.13), channel_id=1, source_target_pairs={{0,1},{1,2},{2,3},{4,5},{5,6},{6,7},{8,9},{9,10},{10,11},{12,13},{... | collective-permute-start | bytes 49160 | tf_op jit(solution)/shard_map/ppermute | solution.py:23
  21.9 5.1 %collective-permute-start.5 = (f32[4,1,1024]{2,0,1:T(4,128)S(1)}, f32[4,1,1024]{2,0,1:T(4,128)S(1)}, u32[]{:S(2)}, u32[]{:S(2)}) collective-permute-start(f32[4,1,1024]{2,0,1:T(4,128)S(1)} %get-tuple-element.14), channel_id=1, source_target_pairs={{1,0},{2,1},{3,2},{5,4},{6,5},{7,6},{9,8},{10,9},{11,10},{13,12},{... | collective-permute-start | bytes 49160 | tf_op jit(solution)/shard_map/ppermute | solution.py:25
  27.2 12.6 %collective-permute-start.6 = (f32[4,1,1024]{2,0,1:T(4,128)S(1)}, f32[4,1,1024]{2,0,1:T(4,128)S(1)}, u32[]{:S(2)}, u32[]{:S(2)}) collective-permute-start(f32[4,1,1024]{2,0,1:T(4,128)S(1)} %get-tuple-element.11), channel_id=1, source_target_pairs={{0,1},{1,2},{2,3},{4,5},{5,6},{6,7},{8,9},{9,10},{10,11},{12,13},{... | collective-permute-start | bytes 49160 | tf_op jit(solution)/shard_map/ppermute | solution.py:23
  29.1 10.7 %collective-permute-start.7 = (f32[4,1,1024]{2,0,1:T(4,128)S(1)}, f32[4,1,1024]{2,0,1:T(4,128)S(1)}, u32[]{:S(2)}, u32[]{:S(2)}) collective-permute-start(f32[4,1,1024]{2,0,1:T(4,128)S(1)} %get-tuple-element.12), channel_id=1, source_target_pairs={{1,0},{2,1},{3,2},{5,4},{6,5},{7,6},{9,8},{10,9},{11,10},{13,12},{... | collective-permute-start | bytes 49160 | tf_op jit(solution)/shard_map/ppermute | solution.py:25
  43.3 11.2 %all-to-all-start = ((bf16[8,2,1024]{2,1,0:T(2,128)(2,1)}), bf16[8,2,1024]{2,1,0:T(2,128)(2,1)S(1)}, u32[]{:S(2)}, u32[]{:S(2)}) async-start(bf16[8,2,1024]{2,1,0:T(2,128)(2,1)} %reshape.227), calls=%async_computation | async-start | bytes 65536 | tf_op jit(solution)/shard_map/all_to_all | solution.py:143
  59.2 0.7 copy-start.4
  59.2 0.7 copy-start.3
  60.0 3.7 %collective-permute-start.8 = (f32[1,1,20,256]{3,2,1,0:T(8,128)S(1)}, f32[1,1,20,256]{3,2,1,0:T(8,128)S(1)}, u32[]{:S(2)}, u32[]{:S(2)}) collective-permute-start(f32[1,1,20,256]{3,2,1,0:T(8,128)S(1)} %bitcast.132), channel_id=1, source_target_pairs={{0,4},{4,8},{8,12},{12,16},{16,20},{20,24},{24,28},{1,5},{5,9},{9,... | collective-permute-start | bytes 61448 | tf_op jit(solution)/shard_map/ppermute | solution.py:23
  62.3 4.6 %collective-permute-start.9 = (f32[1,1,20,256]{3,2,1,0:T(8,128)S(1)}, f32[1,1,20,256]{3,2,1,0:T(8,128)S(1)}, u32[]{:S(2)}, u32[]{:S(2)}) collective-permute-start(f32[1,1,20,256]{3,2,1,0:T(8,128)S(1)} %bitcast.133), channel_id=1, source_target_pairs={{4,0},{8,4},{12,8},{16,12},{20,16},{24,20},{28,24},{5,1},{9,5},{13... | collective-permute-start | bytes 61448 | tf_op jit(solution)/shard_map/ppermute | solution.py:25
  66.9 7.7 %collective-permute-start.10 = (f32[1,3,20,256]{3,0,2,1:T(1,128)S(1)}, f32[1,3,20,256]{3,0,2,1:T(1,128)S(1)}, u32[]{:S(2)}, u32[]{:S(2)}) collective-permute-start(f32[1,3,20,256]{3,0,2,1:T(1,128)S(1)} %copy_dynamic-update-slice_fusion), channel_id=1, source_target_pairs={{0,1},{1,2},{2,3},{4,5},{5,6},{6,7},{8,9},{9,10},{10,11},{12,13},{... | collective-permute-start | bytes 184328 | tf_op jit(solution)/shard_map/ppermute | solution.py:23
  72.6 5.5 %collective-permute-start.11 = (f32[1,3,20,256]{3,0,2,1:T(1,128)S(1)}, f32[1,3,20,256]{3,0,2,1:T(1,128)S(1)}, u32[]{:S(2)}, u32[]{:S(2)}) collective-permute-start(f32[1,3,20,256]{3,0,2,1:T(1,128)S(1)} %copy_dynamic-update-slice_fusion), channel_id=1, source_target_pairs={{1,0},{2,1},{3,2},{5,4},{6,5},{7,6},{9,8},{10,9},{11,10},{13,12},{... | collective-permute-start | bytes 184328 | tf_op jit(solution)/shard_map/ppermute | solution.py:25
where the time goes:
time: 94 us; the launch traced here: 93.3 us
  starting transfers between devices  37.4 us (40%)
  local copies, waits for them, and re-layouts  21 us (22%)
  waiting for transfers between devices  18.1 us (19%)
  blocking collectives  8.78 us (9%)
  matrix products  5.2 us (6%)
  other arithmetic  2.15 us (2%)
    ppermute x6, starting transfers between devices, with_halo(): lax.ppermute(tail, axis, [(i, (i + 1) % count) for i in range(ends)])  20 us
    unnamed x28, local copies, waits for them, and re-layouts  16.8 us
    ppermute x6, waiting for transfers between devices, with_halo(): lax.ppermute(head, axis, [((i + 1) % count, i) for i in range(ends)])  12.4 us
    ppermute x6, starting transfers between devices, with_halo(): lax.ppermute(head, axis, [((i + 1) % count, i) for i in range(ends)])  11.8 us
    all_to_all x1, blocking collectives, on_device(): lax.all_to_all(updated, 'mem', split_axis=0, concat_axis=3, tiled=True)  8.78 us
    all_to_all x1, waiting for transfers between devices, on_device(): lax.all_to_all(predict_advance, 'mem', split_axis=3, concat_axis=0, tiled...  5.62 us
    all_to_all x1, starting transfers between devices, on_device(): lax.all_to_all(predict_advance, 'mem', split_axis=3, concat_axis=0, tiled...  5.55 us
  transfers between devices with their start and end apart: 13, of which 5 were waited for; matrix products, arithmetic and copies ran while one was open for 9% of the time, Pallas kernels for 0%

commit v1 on v0

--- a/solution.py
+++ b/solution.py
@@ -10,6 +10,29 @@
 LOC_COLS = 64
 KAPPA = (0.025, 0.0125)
 HIGHEST = lax.Precision.HIGHEST
+
+
+def split_up(value, dim, count):
+    before, after = (value.shape[:dim], value.shape[dim + 1 :])
+    return jnp.moveaxis(value.reshape(*before, count, -1, *after), dim, 0)
+
+
+def joined_along(parts, dim):
+    parts = jnp.moveaxis(parts, 0, dim)
+    dims = parts.shape
+    return parts.reshape(*dims[:dim], dims[dim] * dims[dim + 1], *dims[dim + 2 :])
+
+
+def rotated_exchange(array, axis, split_dim, concat_dim):
+    size, index = (lax.axis_size(axis), lax.axis_index(axis))
+    parts = split_up(array, split_dim, size)
+    out = parts
+    for step in range(1, size):
+        target, source = ((index + step) % size, (index - step) % size)
+        sent = lax.dynamic_index_in_dim(parts, target, 0)
+        other = lax.ppermute(sent, axis, [(i, (i + step) % size) for i in range(size)])
+        out = lax.dynamic_update_slice_in_dim(out, other, source, axis=0)
+    return joined_along(out, concat_dim)
 
 
 def with_halo(cells, sides, width):
@@ -140,7 +163,7 @@
         ],
         axis=0,
     )
-    mesh_patches = lax.all_to_all(predict_advance, "mem", split_axis=3, concat_axis=0, tiled=True)
+    mesh_patches = rotated_exchange(predict_advance, "mem", 3, 0)
     sample_realizations = mesh_patches.shape[0]
     own_obs = jnp.take(mesh_patches[:, 0].reshape(sample_realizations, -1), cells, axis=1).astype(
         jnp.float32

time: 94 us -> 86.3 us (0.918)
  the two profiles are of different devices: /device:TPU:1 before, /device:TPU:2 now
where the time goes in v1:
time: 86.3 us; the launch traced here: 85.6 us
  starting transfers between devices  43.5 us (50%)
  local copies, waits for them, and re-layouts  13.3 us (15%)
  blocking collectives  11.7 us (14%)
  waiting for transfers between devices  8.88 us (10%)
  matrix products  5.19 us (6%)
  other arithmetic  2.22 us (3%)
  between operations  0.87 us (1%)
    ppermute x6, starting transfers between devices, with_halo(): lax.ppermute(head, axis, [((i + 1) % count, i) for i in range(ends)])  16.1 us
    ppermute x6, starting transfers between devices, with_halo(): lax.ppermute(tail, axis, [(i, (i + 1) % count) for i in range(ends)])  15.1 us
    ppermute x7, starting transfers between devices, rotated_exchange(): lax.ppermute(sent, axis, [(i, (i + step) % size) for i in range(size)])  12.3 us
    all_to_all x1, blocking collectives, on_device(): lax.all_to_all(updated, 'mem', split_axis=0, concat_axis=3, tiled=True)  11.7 us
    unnamed x28, local copies, waits for them, and re-layouts  10.7 us
    ppermute x6, waiting for transfers between devices, with_halo(): lax.ppermute(tail, axis, [(i, (i + 1) % count) for i in range(ends)])  4.75 us
    ppermute x6, waiting for transfers between devices, with_halo(): lax.ppermute(head, axis, [((i + 1) % count, i) for i in range(ends)])  4.1 us
  transfers between devices with their start and end apart: 19, of which 6 were waited for; matrix products, arithmetic and copies ran while one was open for 11% of the time, Pallas kernels for 0%

profile of v1, /device:TPU:2, one launch (start us, length us, event | category | flops | bytes accessed | tf_op | source)
XLA Modules:
  0.0 85.6 jit_solution(15083743646276781989)
XLA Ops:
  0.0 0.8 bitcast_convert_fusion
  0.8 1.9 %collective-permute-start.1 = (f32[4,1,1024]{2,1,0:T(1,128)S(1)}, f32[4,1,1024]{2,1,0:T(1,128)S(1)}, u32[]{:S(2)}, u32[]{:S(2)}) collective-permute-start(f32[4,1,1024]{2,1,0:T(1,128)S(1)} %get-tuple-element.17), channel_id=1, source_target_pairs={{1,0},{2,1},{3,2},{5,4},{6,5},{7,6},{9,8},{10,9},{11,10},{13,12},{... | collective-permute-start | bytes 49160 | tf_op jit(solution)/shard_map/ppermute | solution.py:48
  2.7 2.4 %collective-permute-start = (f32[4,1,1024]{2,1,0:T(1,128)S(1)}, f32[4,1,1024]{2,1,0:T(1,128)S(1)}, u32[]{:S(2)}, u32[]{:S(2)}) collective-permute-start(f32[4,1,1024]{2,1,0:T(1,128)S(1)} %get-tuple-element.18), channel_id=1, source_target_pairs={{0,1},{1,2},{2,3},{4,5},{5,6},{6,7},{8,9},{9,10},{10,11},{12,13},{... | collective-permute-start | bytes 49160 | tf_op jit(solution)/shard_map/ppermute | solution.py:46
  5.3 0.6 copy-done.7
  5.9 0.1 and_reduce_fusion
  6.1 0.6 copy-done.6
  6.9 0.6 copy-done.9
  7.6 0.2 collective-permute-done
  7.8 0.2 fusion.20
  8.0 1.9 %collective-permute-start.2 = (f32[4,1,1024]{2,1,0:T(1,128)S(1)}, f32[4,1,1024]{2,1,0:T(1,128)S(1)}, u32[]{:S(2)}, u32[]{:S(2)}) collective-permute-start(f32[4,1,1024]{2,1,0:T(1,128)S(1)} %get-tuple-element.15), channel_id=1, source_target_pairs={{0,1},{1,2},{2,3},{4,5},{5,6},{6,7},{8,9},{9,10},{10,11},{12,13},{... | collective-permute-start | bytes 49160 | tf_op jit(solution)/shard_map/ppermute | solution.py:46
  9.9 3.6 %collective-permute-start.3 = (f32[4,1,1024]{2,1,0:T(1,128)S(1)}, f32[4,1,1024]{2,1,0:T(1,128)S(1)}, u32[]{:S(2)}, u32[]{:S(2)}) collective-permute-start(f32[4,1,1024]{2,1,0:T(1,128)S(1)} %get-tuple-element.16), channel_id=1, source_target_pairs={{1,0},{2,1},{3,2},{5,4},{6,5},{7,6},{9,8},{10,9},{11,10},{13,12},{... | collective-permute-start | bytes 49160 | tf_op jit(solution)/shard_map/ppermute | solution.py:48
  13.6 1.4 %collective-permute-done.3 = f32[4,1,1024]{2,1,0:T(1,128)S(1)} collective-permute-done((f32[4,1,1024]{2,1,0:T(1,128)S(1)}, f32[4,1,1024]{2,1,0:T(1,128)S(1)}, u32[]{:S(2)}, u32[]{:S(2)}) %collective-permute-start.3) | collective-permute-done | bytes 16416 | tf_op jit(solution)/shard_map/ppermute | solution.py:48
  15.0 0.2 fusion.55
  15.2 1.9 %collective-permute-start.4 = (f32[4,1,1024]{2,1,0:T(1,128)S(1)}, f32[4,1,1024]{2,1,0:T(1,128)S(1)}, u32[]{:S(2)}, u32[]{:S(2)}) collective-permute-start(f32[4,1,1024]{2,1,0:T(1,128)S(1)} %get-tuple-element.13), channel_id=1, source_target_pairs={{0,1},{1,2},{2,3},{4,5},{5,6},{6,7},{8,9},{9,10},{10,11},{12,13},{... | collective-permute-start | bytes 49160 | tf_op jit(solution)/shard_map/ppermute | solution.py:46
  17.1 3.6 %collective-permute-start.5 = (f32[4,1,1024]{2,1,0:T(1,128)S(1)}, f32[4,1,1024]{2,1,0:T(1,128)S(1)}, u32[]{:S(2)}, u32[]{:S(2)}) collective-permute-start(f32[4,1,1024]{2,1,0:T(1,128)S(1)} %get-tuple-element.14), channel_id=1, source_target_pairs={{1,0},{2,1},{3,2},{5,4},{6,5},{7,6},{9,8},{10,9},{11,10},{13,12},{... | collective-permute-start | bytes 49160 | tf_op jit(solution)/shard_map/ppermute | solution.py:48
  20.8 1.4 %collective-permute-done.5 = f32[4,1,1024]{2,1,0:T(1,128)S(1)} collective-permute-done((f32[4,1,1024]{2,1,0:T(1,128)S(1)}, f32[4,1,1024]{2,1,0:T(1,128)S(1)}, u32[]{:S(2)}, u32[]{:S(2)}) %collective-permute-start.5) | collective-permute-done | bytes 16416 | tf_op jit(solution)/shard_map/ppermute | solution.py:48
  22.2 0.2 fusion.42
  22.4 1.9 %collective-permute-start.6 = (f32[4,1,1024]{2,1,0:T(1,128)S(1)}, f32[4,1,1024]{2,1,0:T(1,128)S(1)}, u32[]{:S(2)}, u32[]{:S(2)}) collective-permute-start(f32[4,1,1024]{2,1,0:T(1,128)S(1)} %get-tuple-element.11), channel_id=1, source_target_pairs={{0,1},{1,2},{2,3},{4,5},{5,6},{6,7},{8,9},{9,10},{10,11},{12,13},{... | collective-permute-start | bytes 49160 | tf_op jit(solution)/shard_map/ppermute | solution.py:46
  24.3 3.6 %collective-permute-start.7 = (f32[4,1,1024]{2,1,0:T(1,128)S(1)}, f32[4,1,1024]{2,1,0:T(1,128)S(1)}, u32[]{:S(2)}, u32[]{:S(2)}) collective-permute-start(f32[4,1,1024]{2,1,0:T(1,128)S(1)} %get-tuple-element.12), channel_id=1, source_target_pairs={{1,0},{2,1},{3,2},{5,4},{6,5},{7,6},{9,8},{10,9},{11,10},{13,12},{... | collective-permute-start | bytes 49160 | tf_op jit(solution)/shard_map/ppermute | solution.py:48
  28.1 1.3 %collective-permute-done.7 = f32[4,1,1024]{2,1,0:T(1,128)S(1)} collective-permute-done((f32[4,1,1024]{2,1,0:T(1,128)S(1)}, f32[4,1,1024]{2,1,0:T(1,128)S(1)}, u32[]{:S(2)}, u32[]{:S(2)}) %collective-permute-start.7) | collective-permute-done | bytes 16416 | tf_op jit(solution)/shard_map/ppermute | solution.py:48
  29.4 0.2 fusion.64
  29.7 1.6 %collective-permute-start.9 = (bf16[1,2,2,4,128]{4,0,3,2,1:T(2,128)(2,1)S(1)}, bf16[1,2,2,4,128]{4,0,3,2,1:T(2,128)(2,1)S(1)}, u32[]{:S(2)}, u32[]{:S(2)}) collective-permute-start(bf16[1,2,2,4,128]{4,0,3,2,1:T(2,128)(2,1)S(1)} %get-tuple-element.28), channel_id=1, source_target_pairs={{0,8},{4,12},{8,16},{12,20},{16,24},{20,28},{24,0},{28,4},{1,9},{5... | collective-permute-start | bytes 12296 | tf_op jit(solution)/shard_map/ppermute | solution.py:33
  31.3 1.5 %collective-permute-start.8 = (bf16[1,2,2,4,128]{4,0,3,2,1:T(2,128)(2,1)S(1)}, bf16[1,2,2,4,128]{4,0,3,2,1:T(2,128)(2,1)S(1)}, u32[]{:S(2)}, u32[]{:S(2)}) collective-permute-start(bf16[1,2,2,4,128]{4,0,3,2,1:T(2,128)(2,1)S(1)} %get-tuple-element.29), channel_id=1, source_target_pairs={{0,4},{4,8},{8,12},{12,16},{16,20},{20,24},{24,28},{28,0},{1,5},{5... | collective-permute-start | bytes 12296 | tf_op jit(solution)/shard_map/ppermute | solution.py:33
  32.8 2.2 %collective-permute-start.12 = (bf16[1,2,2,4,128]{4,0,3,2,1:T(2,128)(2,1)S(1)}, bf16[1,2,2,4,128]{4,0,3,2,1:T(2,128)(2,1)S(1)}, u32[]{:S(2)}, u32[]{:S(2)}) collective-permute-start(bf16[1,2,2,4,128]{4,0,3,2,1:T(2,128)(2,1)S(1)} %get-tuple-element.25), channel_id=1, source_target_pairs={{0,20},{4,24},{8,28},{12,0},{16,4},{20,8},{24,12},{28,16},{1,21},{... | collective-permute-start | bytes 12296 | tf_op jit(solution)/shard_map/ppermute | solution.py:33
  35.0 0.7 collective-permute-start.10
  35.8 2.6 %collective-permute-start.11 = (bf16[1,2,2,4,128]{4,0,3,2,1:T(2,128)(2,1)S(1)}, bf16[1,2,2,4,128]{4,0,3,2,1:T(2,128)(2,1)S(1)}, u32[]{:S(2)}, u32[]{:S(2)}) collective-permute-start(bf16[1,2,2,4,128]{4,0,3,2,1:T(2,128)(2,1)S(1)} %get-tuple-element.26), channel_id=1, source_target_pairs={{0,16},{4,20},{8,24},{12,28},{16,0},{20,4},{24,8},{28,12},{1,17},{... | collective-permute-start | bytes 12296 | tf_op jit(solution)/shard_map/ppermute | solution.py:33
  38.4 1.5 %collective-permute-start.13 = (bf16[1,2,2,4,128]{4,0,3,2,1:T(2,128)(2,1)S(1)}, bf16[1,2,2,4,128]{4,0,3,2,1:T(2,128)(2,1)S(1)}, u32[]{:S(2)}, u32[]{:S(2)}) collective-permute-start(bf16[1,2,2,4,128]{4,0,3,2,1:T(2,128)(2,1)S(1)} %get-tuple-element.24), channel_id=1, source_target_pairs={{0,24},{4,28},{8,0},{12,4},{16,8},{20,12},{24,16},{28,20},{1,25},{... | collective-permute-start | bytes 12296 | tf_op jit(solution)/shard_map/ppermute | solution.py:33
  39.8 2.2 %collective-permute-start.14 = (bf16[1,2,2,4,128]{4,0,3,2,1:T(2,128)(2,1)S(1)}, bf16[1,2,2,4,128]{4,0,3,2,1:T(2,128)(2,1)S(1)}, u32[]{:S(2)}, u32[]{:S(2)}) collective-permute-start(bf16[1,2,2,4,128]{4,0,3,2,1:T(2,128)(2,1)S(1)} %get-tuple-element.23), channel_id=1, source_target_pairs={{0,28},{4,0},{8,4},{12,8},{16,12},{20,16},{24,20},{28,24},{1,29},{... | collective-permute-start | bytes 12296 | tf_op jit(solution)/shard_map/ppermute | solution.py:33
  42.0 8.1 %scatter_custom_fusion = f32[5120]{0:T(1024)S(1)} fusion(s32[2048]{0:T(1024)S(1)} %bitcast.152, f32[2048]{0:T(1024)S(1)} %bitcast.153, f32[]{:T(128)} %constant.165.clone.1), kind=kCustom, calls=%fused_computation.137 | custom fusion | bytes 20484
  50.7 0.1 copy.84
  50.9 0.9 %gather_fusion = bf16[256,16]{1,0:T(8,128)(2,1)S(1)} fusion(bf16[16,512]{0,1:T(8,128)(2,1)S(1)} %bitcast.140, s32[1024]{0:T(1024)S(1)} %pad_clamp_fusion), kind=kCustom, calls=%fused_computation | custom fusion | bytes 17408 | tf_op jit(solution)/shard_map/jit(_take)/gather | solution.py:168
  51.7 0.1 convert_bitcast_fusion
  51.9 0.6 copy-done.5
  52.6 1.3 %collective-permute-start.16 = (f32[1,1,20,256]{3,2,1,0:T(8,128)S(1)}, f32[1,1,20,256]{3,2,1,0:T(8,128)S(1)}, u32[]{:S(2)}, u32[]{:S(2)}) collective-permute-start(f32[1,1,20,256]{3,2,1,0:T(8,128)S(1)} %bitcast.141), channel_id=1, source_target_pairs={{4,0},{8,4},{12,8},{16,12},{20,16},{24,20},{28,24},{5,1},{9,5},{13... | collective-permute-start | bytes 61448 | tf_op jit(solution)/shard_map/ppermute | solution.py:48
  53.9 4.5 %collective-permute-start.15 = (f32[1,1,20,256]{3,2,1,0:T(8,128)S(1)}, f32[1,1,20,256]{3,2,1,0:T(8,128)S(1)}, u32[]{:S(2)}, u32[]{:S(2)}) collective-permute-start(f32[1,1,20,256]{3,2,1,0:T(8,128)S(1)} %bitcast.142), channel_id=1, source_target_pairs={{0,4},{4,8},{8,12},{12,16},{16,20},{20,24},{24,28},{1,5},{5,9},{9,... | collective-permute-start | bytes 61448 | tf_op jit(solution)/shard_map/ppermute | solution.py:46
  58.5 1.5 %collective-permute-done.15 = f32[1,1,20,256]{3,2,1,0:T(8,128)S(1)} collective-permute-done((f32[1,1,20,256]{3,2,1,0:T(8,128)S(1)}, f32[1,1,20,256]{3,2,1,0:T(8,128)S(1)}, u32[]{:S(2)}, u32[]{:S(2)}) %collective-permute-start.15) | collective-permute-done | bytes 20512 | tf_op jit(solution)/shard_map/ppermute | solution.py:46
  60.1 1.9 %collective-permute-start.18 = (f32[1,3,20,256]{3,0,2,1:T(1,128)S(1)}, f32[1,3,20,256]{3,0,2,1:T(1,128)S(1)}, u32[]{:S(2)}, u32[]{:S(2)}) collective-permute-start(f32[1,3,20,256]{3,0,2,1:T(1,128)S(1)} %copy_dynamic-update-slice_fusion), channel_id=1, source_target_pairs={{1,0},{2,1},{3,2},{5,4},{6,5},{7,6},{9,8},{10,9},{11,10},{13,12},{... | collective-permute-start | bytes 184328 | tf_op jit(solution)/shard_map/ppermute | solution.py:48
  62.0 2.4 %collective-permute-start.17 = (f32[1,3,20,256]{3,0,2,1:T(1,128)S(1)}, f32[1,3,20,256]{3,0,2,1:T(1,128)S(1)}, u32[]{:S(2)}, u32[]{:S(2)}) collective-permute-start(f32[1,3,20,256]{3,0,2,1:T(1,128)S(1)} %copy_dynamic-update-slice_fusion), channel_id=1, source_target_pairs={{0,1},{1,2},{2,3},{4,5},{5,6},{6,7},{8,9},{9,10},{10,11},{12,13},{... | collective-permute-start | bytes 184328 | tf_op jit(solution)/shard_map/ppermute | solution.py:46
  64.5 3.0 %collective-permute-done.17 = f32[1,3,20,256]{3,0,2,1:T(1,128)S(1)} collective-permute-done((f32[1,3,20,256]{3,0,2,1:T(1,128)S(1)}, f32[1,3,20,256]{3,0,2,1:T(1,128)S(1)}, u32[]{:S(2)}, u32[]{:S(2)}) %collective-permute-start.17) | collective-permute-done | bytes 61472 | tf_op jit(solution)/shard_map/ppermute | solution.py:46
  67.8 1.3 %abs_reduce_fusion = (f32[4,16]{1,0:T(4,128)S(1)}, f32[4,16,16]{1,2,0:T(8,128)S(1)}) fusion(f32[16,1280]{1,0:T(8,128)S(1)} %slice_subtract_fusion, f32[4,1280]{1,0:T(4,128)S(1)} %multiply_multiply_fusion), kind=kOutput, calls=%fused_computation.107 | convolution fusion | flops 15812544 | bytes 106752 | tf_op jit(solution)/shard_map/rek,fk->ref/dot_general | solution.py:116
  69.1 0.1 reduce_max.9
  69.2 0.3 fusion.7
  69.5 0.3 fusion.94
  69.8 0.2 fusion.73
  70.0 0.2 fusion.6
  70.1 0.2 fusion.100
  70.3 0.2 fusion.99
  70.5 0.2 fusion.5
  70.6 0.2 fusion.102
  70.8 0.2 fusion.101
  71.0 0.2 fusion.4
  71.2 0.2 fusion.104
  71.3 0.2 fusion.103
  71.5 0.2 fusion.3
  71.7 0.2 fusion.105
  71.8 0.2 fusion.106
  72.0 0.2 fusion.69
  72.2 0.2 fusion.2
  72.4 0.2 convolution_divide_fusion
  72.6 0.2 convolution_bitcast_fusion.1
  72.7 0.2 fusion.107
  72.9 0.3 fusion.1
  73.3 11.7 %all_to_all.18 = bf16[16,2,4,128]{3,1,2,0:T(2,128)(2,1)S(1)} all-to-all(bf16[16,2,4,128]{3,1,2,0:T(2,128)(2,1)S(1)} %copy.75), channel_id=1, replica_groups=mesh['mem'=8,'lat'=4] {'mem'}, dimensions={0} | all-to-all | bytes 65536 | tf_op jit(solution)/shard_map/all_to_all | solution.py:191
  85.0 0.6 all_to_all.16
  (96 shorter events, 1.7 us)
Async XLA Ops:
  0.8 4.4 %copy-start.2 = (s32[1,256]{1,0:T(1,128)S(1)}, s32[1,256]{1,0:T(1,128)}, u32[]{:S(2)}) copy-start(s32[1,256]{1,0:T(1,128)} %param.10) | copy-start | bytes 3076
  0.8 4.4 %copy-start.3 = (s32[4,1,512]{2,1,0:T(1,128)S(1)}, s32[4,1,512]{2,1,0:T(1,128)}, u32[]{:S(2)}) copy-start(s32[4,1,512]{2,1,0:T(1,128)} %param.13) | copy-start | bytes 24580
  0.8 6.8 %collective-permute-start.1 = (f32[4,1,1024]{2,1,0:T(1,128)S(1)}, f32[4,1,1024]{2,1,0:T(1,128)S(1)}, u32[]{:S(2)}, u32[]{:S(2)}) collective-permute-start(f32[4,1,1024]{2,1,0:T(1,128)S(1)} %get-tuple-element.17), channel_id=1, source_target_pairs={{1,0},{2,1},{3,2},{5,4},{6,5},{7,6},{9,8},{10,9},{11,10},{13,12},{... | collective-permute-start | bytes 49160 | tf_op jit(solution)/shard_map/ppermute | solution.py:48
  2.7 5.1 %collective-permute-start = (f32[4,1,1024]{2,1,0:T(1,128)S(1)}, f32[4,1,1024]{2,1,0:T(1,128)S(1)}, u32[]{:S(2)}, u32[]{:S(2)}) collective-permute-start(f32[4,1,1024]{2,1,0:T(1,128)S(1)} %get-tuple-element.18), channel_id=1, source_target_pairs={{0,1},{1,2},{2,3},{4,5},{5,6},{6,7},{8,9},{9,10},{10,11},{12,13},{... | collective-permute-start | bytes 49160 | tf_op jit(solution)/shard_map/ppermute | solution.py:46
  5.2 0.7 copy-start.7
  5.2 0.8 copy-start.8
  5.3 1.6 %copy-start.1 = (f32[2,4,1024]{2,1,0:T(4,128)S(1)}, f32[2,4,1024]{2,1,0:T(4,128)}, u32[]{:S(2)}) copy-start(f32[2,4,1024]{2,1,0:T(4,128)} %param.9) | copy-start | bytes 98308
  6.1 0.7 copy-start.6
  6.8 0.7 copy-start.9
  6.8 1.0 %copy-start = (bf16[2,2,4,1024]{3,2,1,0:T(4,128)(2,1)S(1)}, bf16[2,2,4,1024]{3,2,1,0:T(4,128)(2,1)}, u32[]{:S(2)}) copy-start(bf16[2,2,4,1024]{3,2,1,0:T(4,128)(2,1)} %param.8) | copy-start | bytes 98308
  8.0 5.6 %collective-permute-start.2 = (f32[4,1,1024]{2,1,0:T(1,128)S(1)}, f32[4,1,1024]{2,1,0:T(1,128)S(1)}, u32[]{:S(2)}, u32[]{:S(2)}) collective-permute-start(f32[4,1,1024]{2,1,0:T(1,128)S(1)} %get-tuple-element.15), channel_id=1, source_target_pairs={{0,1},{1,2},{2,3},{4,5},{5,6},{6,7},{8,9},{9,10},{10,11},{12,13},{... | collective-permute-start | bytes 49160 | tf_op jit(solution)/shard_map/ppermute | solution.py:46
  9.9 5.1 %collective-permute-start.3 = (f32[4,1,1024]{2,1,0:T(1,128)S(1)}, f32[4,1,1024]{2,1,0:T(1,128)S(1)}, u32[]{:S(2)}, u32[]{:S(2)}) collective-permute-start(f32[4,1,1024]{2,1,0:T(1,128)S(1)} %get-tuple-element.16), channel_id=1, source_target_pairs={{1,0},{2,1},{3,2},{5,4},{6,5},{7,6},{9,8},{10,9},{11,10},{13,12},{... | collective-permute-start | bytes 49160 | tf_op jit(solution)/shard_map/ppermute | solution.py:48
  15.2 5.6 %collective-permute-start.4 = (f32[4,1,1024]{2,1,0:T(1,128)S(1)}, f32[4,1,1024]{2,1,0:T(1,128)S(1)}, u32[]{:S(2)}, u32[]{:S(2)}) collective-permute-start(f32[4,1,1024]{2,1,0:T(1,128)S(1)} %get-tuple-element.13), channel_id=1, source_target_pairs={{0,1},{1,2},{2,3},{4,5},{5,6},{6,7},{8,9},{9,10},{10,11},{12,13},{... | collective-permute-start | bytes 49160 | tf_op jit(solution)/shard_map/ppermute | solution.py:46
  17.1 5.1 %collective-permute-start.5 = (f32[4,1,1024]{2,1,0:T(1,128)S(1)}, f32[4,1,1024]{2,1,0:T(1,128)S(1)}, u32[]{:S(2)}, u32[]{:S(2)}) collective-permute-start(f32[4,1,1024]{2,1,0:T(1,128)S(1)} %get-tuple-element.14), channel_id=1, source_target_pairs={{1,0},{2,1},{3,2},{5,4},{6,5},{7,6},{9,8},{10,9},{11,10},{13,12},{... | collective-permute-start | bytes 49160 | tf_op jit(solution)/shard_map/ppermute | solution.py:48
  22.4 5.7 %collective-permute-start.6 = (f32[4,1,1024]{2,1,0:T(1,128)S(1)}, f32[4,1,1024]{2,1,0:T(1,128)S(1)}, u32[]{:S(2)}, u32[]{:S(2)}) collective-permute-start(f32[4,1,1024]{2,1,0:T(1,128)S(1)} %get-tuple-element.11), channel_id=1, source_target_pairs={{0,1},{1,2},{2,3},{4,5},{5,6},{6,7},{8,9},{9,10},{10,11},{12,13},{... | collective-permute-start | bytes 49160 | tf_op jit(solution)/shard_map/ppermute | solution.py:46
  24.3 5.1 %collective-permute-start.7 = (f32[4,1,1024]{2,1,0:T(1,128)S(1)}, f32[4,1,1024]{2,1,0:T(1,128)S(1)}, u32[]{:S(2)}, u32[]{:S(2)}) collective-permute-start(f32[4,1,1024]{2,1,0:T(1,128)S(1)} %get-tuple-element.12), channel_id=1, source_target_pairs={{1,0},{2,1},{3,2},{5,4},{6,5},{7,6},{9,8},{10,9},{11,10},{13,12},{... | collective-permute-start | bytes 49160 | tf_op jit(solution)/shard_map/ppermute | solution.py:48
  29.7 8.7 %collective-permute-start.9 = (bf16[1,2,2,4,128]{4,0,3,2,1:T(2,128)(2,1)S(1)}, bf16[1,2,2,4,128]{4,0,3,2,1:T(2,128)(2,1)S(1)}, u32[]{:S(2)}, u32[]{:S(2)}) collective-permute-start(bf16[1,2,2,4,128]{4,0,3,2,1:T(2,128)(2,1)S(1)} %get-tuple-element.28), channel_id=1, source_target_pairs={{0,8},{4,12},{8,16},{12,20},{16,24},{20,28},{24,0},{28,4},{1,9},{5... | collective-permute-start | bytes 12296 | tf_op jit(solution)/shard_map/ppermute | solution.py:33
  31.3 8.5 %collective-permute-start.8 = (bf16[1,2,2,4,128]{4,0,3,2,1:T(2,128)(2,1)S(1)}, bf16[1,2,2,4,128]{4,0,3,2,1:T(2,128)(2,1)S(1)}, u32[]{:S(2)}, u32[]{:S(2)}) collective-permute-start(bf16[1,2,2,4,128]{4,0,3,2,1:T(2,128)(2,1)S(1)} %get-tuple-element.29), channel_id=1, source_target_pairs={{0,4},{4,8},{8,12},{12,16},{16,20},{20,24},{24,28},{28,0},{1,5},{5... | collective-permute-start | bytes 12296 | tf_op jit(solution)/shard_map/ppermute | solution.py:33
  32.8 17.6 %collective-permute-start.12 = (bf16[1,2,2,4,128]{4,0,3,2,1:T(2,128)(2,1)S(1)}, bf16[1,2,2,4,128]{4,0,3,2,1:T(2,128)(2,1)S(1)}, u32[]{:S(2)}, u32[]{:S(2)}) collective-permute-start(bf16[1,2,2,4,128]{4,0,3,2,1:T(2,128)(2,1)S(1)} %get-tuple-element.25), channel_id=1, source_target_pairs={{0,20},{4,24},{8,28},{12,0},{16,4},{20,8},{24,12},{28,16},{1,21},{... | collective-permute-start | bytes 12296 | tf_op jit(solution)/shard_map/ppermute | solution.py:33
  35.0 15.3 %collective-permute-start.10 = (bf16[1,2,2,4,128]{4,0,3,2,1:T(2,128)(2,1)S(1)}, bf16[1,2,2,4,128]{4,0,3,2,1:T(2,128)(2,1)S(1)}, u32[]{:S(2)}, u32[]{:S(2)}) collective-permute-start(bf16[1,2,2,4,128]{4,0,3,2,1:T(2,128)(2,1)S(1)} %get-tuple-element.27), channel_id=1, source_target_pairs={{0,12},{4,16},{8,20},{12,24},{16,28},{20,0},{24,4},{28,8},{1,13},{... | collective-permute-start | bytes 12296 | tf_op jit(solution)/shard_map/ppermute | solution.py:33
  35.8 14.6 %collective-permute-start.11 = (bf16[1,2,2,4,128]{4,0,3,2,1:T(2,128)(2,1)S(1)}, bf16[1,2,2,4,128]{4,0,3,2,1:T(2,128)(2,1)S(1)}, u32[]{:S(2)}, u32[]{:S(2)}) collective-permute-start(bf16[1,2,2,4,128]{4,0,3,2,1:T(2,128)(2,1)S(1)} %get-tuple-element.26), channel_id=1, source_target_pairs={{0,16},{4,20},{8,24},{12,28},{16,0},{20,4},{24,8},{28,12},{1,17},{... | collective-permute-start | bytes 12296 | tf_op jit(solution)/shard_map/ppermute | solution.py:33
  38.4 12.2 %collective-permute-start.13 = (bf16[1,2,2,4,128]{4,0,3,2,1:T(2,128)(2,1)S(1)}, bf16[1,2,2,4,128]{4,0,3,2,1:T(2,128)(2,1)S(1)}, u32[]{:S(2)}, u32[]{:S(2)}) collective-permute-start(bf16[1,2,2,4,128]{4,0,3,2,1:T(2,128)(2,1)S(1)} %get-tuple-element.24), channel_id=1, source_target_pairs={{0,24},{4,28},{8,0},{12,4},{16,8},{20,12},{24,16},{28,20},{1,25},{... | collective-permute-start | bytes 12296 | tf_op jit(solution)/shard_map/ppermute | solution.py:33
  39.8 10.8 %collective-permute-start.14 = (bf16[1,2,2,4,128]{4,0,3,2,1:T(2,128)(2,1)S(1)}, bf16[1,2,2,4,128]{4,0,3,2,1:T(2,128)(2,1)S(1)}, u32[]{:S(2)}, u32[]{:S(2)}) collective-permute-start(bf16[1,2,2,4,128]{4,0,3,2,1:T(2,128)(2,1)S(1)} %get-tuple-element.23), channel_id=1, source_target_pairs={{0,28},{4,0},{8,4},{12,8},{16,12},{20,16},{24,20},{28,24},{1,29},{... | collective-permute-start | bytes 12296 | tf_op jit(solution)/shard_map/ppermute | solution.py:33
  51.8 0.7 copy-start.5
  51.9 0.7 copy-start.4
  52.6 7.4 %collective-permute-start.16 = (f32[1,1,20,256]{3,2,1,0:T(8,128)S(1)}, f32[1,1,20,256]{3,2,1,0:T(8,128)S(1)}, u32[]{:S(2)}, u32[]{:S(2)}) collective-permute-start(f32[1,1,20,256]{3,2,1,0:T(8,128)S(1)} %bitcast.141), channel_id=1, source_target_pairs={{4,0},{8,4},{12,8},{16,12},{20,16},{24,20},{28,24},{5,1},{9,5},{13... | collective-permute-start | bytes 61448 | tf_op jit(solution)/shard_map/ppermute | solution.py:48
  53.9 6.1 %collective-permute-start.15 = (f32[1,1,20,256]{3,2,1,0:T(8,128)S(1)}, f32[1,1,20,256]{3,2,1,0:T(8,128)S(1)}, u32[]{:S(2)}, u32[]{:S(2)}) collective-permute-start(f32[1,1,20,256]{3,2,1,0:T(8,128)S(1)} %bitcast.142), channel_id=1, source_target_pairs={{0,4},{4,8},{8,12},{12,16},{16,20},{20,24},{24,28},{1,5},{5,9},{9,... | collective-permute-start | bytes 61448 | tf_op jit(solution)/shard_map/ppermute | solution.py:46
  60.1 4.4 %collective-permute-start.18 = (f32[1,3,20,256]{3,0,2,1:T(1,128)S(1)}, f32[1,3,20,256]{3,0,2,1:T(1,128)S(1)}, u32[]{:S(2)}, u32[]{:S(2)}) collective-permute-start(f32[1,3,20,256]{3,0,2,1:T(1,128)S(1)} %copy_dynamic-update-slice_fusion), channel_id=1, source_target_pairs={{1,0},{2,1},{3,2},{5,4},{6,5},{7,6},{9,8},{10,9},{11,10},{13,12},{... | collective-permute-start | bytes 184328 | tf_op jit(solution)/shard_map/ppermute | solution.py:48
  62.0 5.5 %collective-permute-start.17 = (f32[1,3,20,256]{3,0,2,1:T(1,128)S(1)}, f32[1,3,20,256]{3,0,2,1:T(1,128)S(1)}, u32[]{:S(2)}, u32[]{:S(2)}) collective-permute-start(f32[1,3,20,256]{3,0,2,1:T(1,128)S(1)} %copy_dynamic-update-slice_fusion), channel_id=1, source_target_pairs={{0,1},{1,2},{2,3},{4,5},{5,6},{6,7},{8,9},{9,10},{10,11},{12,13},{... | collective-permute-start | bytes 184328 | tf_op jit(solution)/shard_map/ppermute | solution.py:46
